TPU v7x, 32 devices: a whole 2x2x4 slice. The times are simulated.
32 devices in a mesh: ep: 8 (over z, y), tp: 4 (over x, core).
Axes of the slice: x: 2, y: 2, z: 4, core: 2. Of those that a mesh axis runs over, the one named last changes fastest.
Arguments:
- tokens_first: bfloat16 [384, 2048], P('ep', 'tp'), may hold values from -6 to 6
- routes_first: int32 [384, 8], P('ep'), may hold values from 0 to 63, all different within a row; in each aligned block of 48 rows (0 to 47, 48 to 95, ...) at most 12 rows name the same one
- weights_first: float32 [384, 8], P('ep'), may hold values from 0.05 to 1
- tokens_second: bfloat16 [384, 2048], P('ep', 'tp'), may hold values from -6 to 6
- stream_second: bfloat16 [384, 2048], P('ep', 'tp'), may hold values from -6 to 6
- routes_second: int32 [384, 8], P('ep'), may hold values from 0 to 63, all different within a row; in each aligned block of 48 rows (0 to 47, 48 to 95, ...) at most 12 rows name the same one
- weights_second: float32 [384, 8], P('ep'), may hold values from 0.05 to 1
- old_place: int32 [64], replicated, may hold values from 0 to 63, each once
- new_place: int32 [72], replicated, may hold values from 0 to 63, as said below
- gate_up: bfloat16 [64, 2, 2048, 1024], P('ep', None, None, 'tp'), may hold values from -0.125 to 0.125
- down_proj: bfloat16 [64, 1024, 2048], P('ep', 'tp'), may hold values from -0.1875 to 0.1875
- attn_gain: float32 [2048], P('tp'), may hold values from 0.25 to 1.75
- qkv_weight: bfloat16 [2048, 3, 2048], P(None, None, 'tp'), may hold values from -0.125 to 0.125
- query_gain: float32 [128], replicated, may hold values from 0.25 to 1.75
- key_gain: float32 [128], replicated, may hold values from 0.25 to 1.75
- positions: int32 [384], P('ep'), may hold values from 0 to 4095
Outputs:
- output_first: bfloat16 [384, 2048], P('ep', 'tp')
- query_rows: bfloat16 [384, 2048], P('ep', 'tp')
- key_rows: bfloat16 [384, 2048], P('ep', 'tp')
- value_rows: bfloat16 [384, 2048], P('ep', 'tp')
- new_gate_up: bfloat16 [72, 2, 2048, 1024], P('ep', None, None, 'tp')
- new_down: bfloat16 [72, 1024, 2048], P('ep', 'tp')
Inputs may be any that keep to these rules, and one draw needn't show every extreme that they name: `routes_first`: within the 48 rows of one index of ep, no expert is named more than 12 times, a bound that some block reaches. `routes_second`: within the 48 rows of one index of ep, no expert is named more than 12 times, a bound that some block reaches. `old_place`: each expert is held by exactly one slot. `new_place`: slots s * 9 to s * 9 + 8 belong to index s of ep; every expert is held by at least one slot, and some by two or more.
All inputs are finite; a program needn't handle non-finite values.
Results may differ from a plain program's by a relative error of at most 0.017.
Values may be sent and summed in bfloat16 or wider, within the bound.
A program may use at most 192 MiB of HBM per device.

v0:
```python
import math

import jax
import jax.numpy as jnp
from jax import lax
from jax.sharding import PartitionSpec as P

D = 2048
EXPERTS = 64
HEAD_DIM = 128
CAP = 12


def place_rows(routes, target_slot, total_slots):
    flattened = routes.reshape(-1)
    experts_range = jnp.arange(target_slot.shape[0], dtype=jnp.int32)
    onehot = (flattened[:, None] == experts_range[None, :]).astype(jnp.int32)
    position = jnp.sum((jnp.cumsum(onehot, axis=0) - 1) * onehot, axis=1)
    slot_index = jnp.sum(onehot * target_slot[None, :], axis=1)
    row_index = slot_index * CAP + position
    owners = jnp.full((total_slots * CAP,), routes.shape[0], jnp.int32)
    owners = owners.at[row_index].set(
        jnp.arange(flattened.shape[0], dtype=jnp.int32) // routes.shape[1]
    )
    return (row_index, owners)


def run_batch(tokens, routes, weights, target_slot, slot_gate_up, slot_down):
    ep_count = lax.axis_size("ep")
    slots_here = slot_gate_up.shape[0]
    row_index, owners = place_rows(routes, target_slot, ep_count * slots_here)
    padded = jnp.concatenate([tokens, jnp.zeros((1, tokens.shape[1]), jnp.bfloat16)], axis=0)
    outgoing = padded[owners].reshape(ep_count, slots_here, CAP, tokens.shape[1])
    features = lax.all_gather(
        lax.all_to_all(outgoing, "ep", split_axis=0, concat_axis=0, tiled=True),
        "tp",
        axis=3,
        tiled=True,
    )
    gate_part = jnp.einsum(
        "secd,edf->secf", features, slot_gate_up[:, 0], preferred_element_type=jnp.float32
    )
    up_part = jnp.einsum(
        "secd,edf->secf", features, slot_gate_up[:, 1], preferred_element_type=jnp.float32
    )
    hidden = (jax.nn.silu(gate_part) * up_part).astype(jnp.bfloat16)
    partial_value = jnp.einsum(
        "secf,efd->secd", hidden, slot_down, preferred_element_type=jnp.float32
    )
    result = lax.psum_scatter(
        partial_value.astype(jnp.bfloat16), "tp", scatter_dimension=3, tiled=True
    )
    returned = lax.all_to_all(result, "ep", split_axis=0, concat_axis=0, tiled=True)
    flat_back = returned.reshape(-1, returned.shape[3])
    picked = flat_back[row_index].astype(jnp.float32).reshape(routes.shape[0], routes.shape[1], -1)
    shares = weights / jnp.sum(weights, axis=1, keepdims=True)
    return jnp.sum(picked * shares[:, :, None], axis=1)


def migrate_first(gate_up, down_proj):
    return (
        lax.all_to_all(gate_up, "ep", split_axis=2, concat_axis=0, tiled=True),
        lax.all_to_all(down_proj, "ep", split_axis=2, concat_axis=0, tiled=True),
    )


def migrate_second(table_gate_up, table_down, new_place, old_slot):
    members = (
        new_place[:, None] == jnp.arange(old_slot.shape[0], dtype=jnp.int32)[None, :]
    ).astype(jnp.int32)
    source = jnp.sum(members * old_slot[None, :], axis=1)
    return (
        lax.all_to_all(table_gate_up[source], "ep", split_axis=0, concat_axis=2, tiled=True),
        lax.all_to_all(table_down[source], "ep", split_axis=0, concat_axis=2, tiled=True),
    )


def head_norm(values, gain):
    mean_sq = jnp.mean(values * values, axis=-1, keepdims=True)
    return values * lax.rsqrt(mean_sq + 1e-06) * gain


def apply_rope(values, positions):
    half = HEAD_DIM // 2
    inverse = jnp.exp(jnp.arange(half, dtype=jnp.float32) * (-2.0 / HEAD_DIM) * math.log(50000.0))
    angle = positions.astype(jnp.float32)[:, None] * inverse[None, :]
    cosine = jnp.cos(angle)[:, None, :]
    sine = jnp.sin(angle)[:, None, :]
    first = values[..., :half]
    second = values[..., half:]
    return jnp.concatenate(
        [first * cosine - second * sine, second * cosine + first * sine], axis=-1
    )


def on_device(
    tokens_first,
    routes_first,
    weights_first,
    tokens_second,
    stream_second,
    routes_second,
    weights_second,
    old_place,
    new_place,
    gate_up,
    down_proj,
    attn_gain,
    qkv_weight,
    query_gain,
    key_gain,
    positions,
):
    experts_range = jnp.arange(EXPERTS, dtype=jnp.int32)
    old_slot = jnp.zeros((EXPERTS,), jnp.int32).at[old_place].set(experts_range)
    table_gate_up, table_down = migrate_first(gate_up, down_proj)
    new_gate_up, new_down = migrate_second(table_gate_up, table_down, new_place, old_slot)
    mixed_first = run_batch(tokens_first, routes_first, weights_first, old_slot, gate_up, down_proj)
    output_first = mixed_first.astype(jnp.bfloat16)
    slot_count = new_place.shape[0]
    members = (new_place[:, None] == experts_range[None, :]).astype(jnp.int32)
    replica_rank = jnp.cumsum(members, axis=0) - 1
    replicas = jnp.sum(members, axis=0)
    wanted = lax.axis_index("ep") % replicas
    chosen = members * (replica_rank == wanted[None, :]).astype(jnp.int32)
    new_target = jnp.sum(chosen * jnp.arange(slot_count, dtype=jnp.int32)[:, None], axis=0)
    mixed_second = run_batch(
        tokens_second, routes_second, weights_second, new_target, new_gate_up, new_down
    )
    stream = stream_second.astype(jnp.float32) + mixed_second
    squares = lax.psum(jnp.sum(stream * stream, axis=1), "tp")
    normed = (stream * lax.rsqrt(squares / D + 1e-06)[:, None] * attn_gain[None, :]).astype(
        jnp.bfloat16
    )
    flat_weight = qkv_weight.reshape(qkv_weight.shape[0], -1)
    tokens_count = normed.shape[0]
    projected = jnp.dot(
        lax.all_gather(normed, "tp", axis=1, tiled=True),
        flat_weight,
        preferred_element_type=jnp.float32,
    )
    heads_here = flat_weight.shape[1] // (3 * HEAD_DIM)
    projected = projected.reshape(tokens_count, 3, heads_here, HEAD_DIM)
    query_heads = head_norm(projected[:, 0], query_gain)
    key_heads = head_norm(projected[:, 1], key_gain)
    query_rows = apply_rope(query_heads, positions).reshape(tokens_count, -1).astype(jnp.bfloat16)
    key_rows = apply_rope(key_heads, positions).reshape(tokens_count, -1).astype(jnp.bfloat16)
    value_rows = projected[:, 2].reshape(tokens_count, -1).astype(jnp.bfloat16)
    return (output_first, query_rows, key_rows, value_rows, new_gate_up, new_down)


def solution(mesh):
    placed = (
        P("ep", "tp"),
        P("ep", None),
        P("ep", None),
        P("ep", "tp"),
        P("ep", "tp"),
        P("ep", None),
        P("ep", None),
        P(),
        P(),
        P("ep", None, None, "tp"),
        P("ep", "tp", None),
        P("tp"),
        P(None, None, "tp"),
        P(),
        P(),
        P("ep"),
    )
    return jax.shard_map(
        on_device,
        mesh=mesh,
        in_specs=placed,
        out_specs=(
            P("ep", "tp"),
            P("ep", "tp"),
            P("ep", "tp"),
            P("ep", "tp"),
            P("ep", None, None, "tp"),
            P("ep", "tp", None),
        ),
        check_vma=False,
    )
```

profile of v0, /device:TPU:0, one launch (start us, length us, event | category | flops | bytes accessed | tf_op | source)
XLA Modules:
  0.0 1415.2 jit_solution(13339023950387459938)
XLA Ops:
  11.0 2.9 scatter_custom_fusion.1
  14.7 2.7 gather_fusion
  17.6 1.3 copy.102
  18.9 7.3 all-to-all-start
  29.0 2.9 scatter_custom_fusion.2
  32.0 3.5 gather_fusion.4
  35.5 1.2 reshape.238
  36.7 9.7 all-to-all-done
  46.4 3.6 all-to-all-start.6
  50.0 12.9 copy.109
  62.8 15.9 %all-to-all-done.6 = bf16[8,9,12,512]{3,2,1,0:T(8,128)(2,1)S(1)} async-done(((bf16[8,9,12,512]{3,2,1,0:T(8,128)(2,1)}), bf16[8,9,12,512]{3,2,1,0:T(8,128)(2,1)S(1)}, u32[]{:S(2)}, u32[]{:S(2)}) %all-to-all-start.6) | async-done | bytes 884768 | tf_op jit(solution)/shard_map/all_to_all | solution.py:35
  78.7 5.0 all-to-all-start.2
  83.7 17.9 %copy.113 = bf16[8,2,2048,256]{3,0,1,2:T(8,128)(2,1)} copy(bf16[8,2,2048,256]{3,2,1,0:T(8,128)(2,1)} %param.25) | data formatting | bytes 33554432 | tf_op args[9]
  101.6 164.5 %all-to-all-done.2 = bf16[8,256,2048]{1,0,2:T(8,128)(2,1)} async-done(((bf16[8,256,2048]{1,0,2:T(8,128)(2,1)}), bf16[8,256,2048]{1,0,2:T(8,128)(2,1)}, u32[]{:S(2)}, u32[]{:S(2)}) %all-to-all-start.2) | async-done | bytes 8388640 | tf_op jit(solution)/shard_map/all_to_all | solution.py:63
  266.1 5.8 all-to-all-start.4
  271.9 12.7 copy.111
  284.6 9.3 gather_fusion.2
  293.9 339.2 %all-to-all-done.4 = bf16[8,2,2048,256]{3,0,1,2:T(8,128)(2,1)} async-done(((bf16[8,2,2048,256]{3,0,1,2:T(8,128)(2,1)}), bf16[8,2,2048,256]{3,0,1,2:T(8,128)(2,1)}, u32[]{:S(2)}, u32[]{:S(2)}) %all-to-all-start.4) | async-done | bytes 16777248 | tf_op jit(solution)/shard_map/all_to_all | solution.py:62
  633.1 5.2 all-to-all-start.3
  638.4 16.0 %copy.115 = bf16[8,8,2,256,256]{4,3,2,1,0:T(8,128)(2,1)} copy(bf16[8,8,2,256,256]{4,1,2,3,0:T(8,128)(2,1)} %bitcast.24) | data formatting | bytes 33554432 | tf_op jit(solution)/shard_map/all_to_all | solution.py:62
  654.3 14.2 %gather_fusion.3 = bf16[72,2,256,256]{3,2,1,0:T(8,128)(2,1)} fusion(bf16[64,2,256,256]{3,2,1,0:T(8,128)(2,1)} %bitcast.182, s32[1024]{0:T(1024)S(1)} %pad_clamp_fusion.2), kind=kCustom, calls=%fused_computation.3 | custom fusion | bytes 37749024 | tf_op jit(solution)/shard_map/gather | solution.py:73
  668.5 174.9 %all-to-all-done.3 = bf16[72,256,256]{2,1,0:T(8,128)(2,1)} async-done(((bf16[72,256,256]{2,1,0:T(8,128)(2,1)}), bf16[72,256,256]{2,1,0:T(8,128)(2,1)}, u32[]{:S(2)}, u32[]{:S(2)}) %all-to-all-start.3) | async-done | bytes 9437216 | tf_op jit(solution)/shard_map/all_to_all | solution.py:74
  843.4 5.9 all-to-all-start.5
  849.4 1.2 copy.103
  851.9 36.2 %all-gather.3.cloned.1.call-done = bf16[8,8,12,2048]{3,2,0,1:T(8,128)(2,1)} async-done(((bf16[8,8,12,512]{3,2,0,1:T(8,128)(2,1)}), bf16[8,8,12,2048]{3,2,0,1:T(8,128)(2,1)}) %all-gather.3.cloned.1.call-update) | async-done | bytes 3145744 | tf_op jit(solution)/shard_map/all_gather | solution.py:34
  888.1 6.0 fusion.19
  894.2 5.7 fusion.29
  900.5 3.3 convert_bitcast_fusion.1
  904.1 13.4 copy.112
  917.5 15.0 %reshape.323 = bf16[9,256,2048,1]{2,1,0,3:T(8,128)(2,1)} reshape(bf16[9,256,8,256]{3,2,1,0:T(8,128)(2,1)} %copy.112) | data formatting | bytes 18874368 | tf_op jit(solution)/shard_map/all_to_all | solution.py:74
  932.5 323.3 %all-to-all-done.5 = bf16[72,2,256,256]{3,2,1,0:T(8,128)(2,1)} async-done(((bf16[72,2,256,256]{3,2,1,0:T(8,128)(2,1)}), bf16[72,2,256,256]{3,2,1,0:T(8,128)(2,1)}, u32[]{:S(2)}, u32[]{:S(2)}) %all-to-all-start.5) | async-done | bytes 18874400 | tf_op jit(solution)/shard_map/all_to_all | solution.py:73
  1255.7 16.7 %copy.116 = bf16[9,2,8,256,256]{4,3,2,0,1:T(8,128)(2,1)} copy(bf16[9,2,8,256,256]{4,3,1,0,2:T(8,128)(2,1)} %bitcast.27) | data formatting | bytes 37748736 | tf_op jit(solution)/shard_map/all_to_all | solution.py:73
  1272.5 6.4 fusion.16
  1278.9 6.6 fusion.28
  1285.5 7.3 convert_bitcast_fusion
  1292.8 2.6 copy.106
  1295.4 4.4 all-to-all-start.1
  1299.9 40.8 %reduce-scatter.5.cloned.1.call-done = bf16[8,9,12,512]{3,2,0,1:T(8,128)(2,1)} async-done(((bf16[8,9,12,2048]{3,2,0,1:T(8,128)(2,1)}), bf16[8,9,12,512]{3,2,0,1:T(8,128)(2,1)}) %reduce-scatter.5.cloned.1.call-update) | async-done | bytes 884752 | tf_op jit(solution)/shard_map/reduce_scatter | solution.py:50
  1340.6 2.5 copy.121
  1343.1 5.5 all-to-all-start.7
  1348.7 8.8 copy.123
  1358.4 2.1 gather_fusion.1
  1361.4 8.8 copy.143
  1370.1 16.5 %copy.127 = bf16[9,2,2048,256]{3,2,1,0:T(8,128)(2,1)} copy(bf16[9,2,2048,256]{3,2,0,1:T(8,128)(2,1)} %bitcast.185) | data formatting | bytes 37748736
  1386.8 2.1 gather_fusion.5
  1389.3 5.9 psum.7
  1395.3 5.6 all_gather.11
  1401.0 4.8 fusion.34
  (114 shorter events, 14.7 us)
Async XLA Ops:
  7.2 19.1 %copy-start.8 = (s32[48,8]{0,1:T(8,128)S(1)}, s32[48,8]{0,1:T(8,128)}, u32[]{:S(2)}) copy-start(s32[48,8]{0,1:T(8,128)} %param.21) | copy-start | bytes 4612
  7.2 20.5 %copy-start.10 = (s32[72]{0:T(128)S(1)}, s32[72]{0:T(128)}, u32[]{:S(2)}) copy-start(s32[72]{0:T(128)} %param.24) | copy-start | bytes 868
  7.2 24.8 %copy-start.1 = (bf16[48,512]{1,0:T(8,128)(2,1)S(1)}, bf16[48,512]{1,0:T(8,128)(2,1)}, u32[]{:S(2)}) copy-start(bf16[48,512]{1,0:T(8,128)(2,1)} %param.19) | copy-start | bytes 147460
  11.0 8.0 copy-start.4
  18.9 27.5 %all-to-all-start = ((bf16[8,8,12,512]{3,1,2,0:T(8,128)(2,1)}), bf16[8,8,12,512]{3,1,2,0:T(8,128)(2,1)S(1)}, u32[]{:S(2)}, u32[]{:S(2)}) async-start(bf16[8,8,12,512]{3,1,2,0:T(8,128)(2,1)} %copy.102), calls=%async_computation | async-start | bytes 1572864 | tf_op jit(solution)/shard_map/all_to_all | solution.py:35
  28.4 0.6 copy-start.6
  46.4 32.3 %all-to-all-start.6 = ((bf16[8,9,12,512]{3,2,1,0:T(8,128)(2,1)}), bf16[8,9,12,512]{3,2,1,0:T(8,128)(2,1)S(1)}, u32[]{:S(2)}, u32[]{:S(2)}) async-start(bf16[8,9,12,512]{3,2,1,0:T(8,128)(2,1)} %reshape.238), calls=%async_computation.7 | async-start | bytes 2359296 | tf_op jit(solution)/shard_map/all_to_all | solution.py:35
  78.7 187.4 %all-to-all-start.2 = ((bf16[8,256,2048]{1,0,2:T(8,128)(2,1)}), bf16[8,256,2048]{1,0,2:T(8,128)(2,1)}, u32[]{:S(2)}, u32[]{:S(2)}) async-start(bf16[8,256,2048]{1,0,2:T(8,128)(2,1)} %copy.109), calls=%async_computation.3 | async-start | bytes 16777216 | tf_op jit(solution)/shard_map/all_to_all | solution.py:63
  266.1 367.0 %all-to-all-start.4 = ((bf16[8,2,2048,256]{3,0,1,2:T(8,128)(2,1)}), bf16[8,2,2048,256]{3,0,1,2:T(8,128)(2,1)}, u32[]{:S(2)}, u32[]{:S(2)}) async-start(bf16[8,2,2048,256]{3,0,1,2:T(8,128)(2,1)} %copy.113), calls=%async_computation.5 | async-start | bytes 33554432 | tf_op jit(solution)/shard_map/all_to_all | solution.py:62
  633.1 210.3 %all-to-all-start.3 = ((bf16[72,256,256]{2,1,0:T(8,128)(2,1)}), bf16[72,256,256]{2,1,0:T(8,128)(2,1)}, u32[]{:S(2)}, u32[]{:S(2)}) async-start(bf16[72,256,256]{2,1,0:T(8,128)(2,1)} %gather_fusion.2), calls=%async_computation.4 | async-start | bytes 18874368 | tf_op jit(solution)/shard_map/all_to_all | solution.py:74
  843.4 412.3 %all-to-all-start.5 = ((bf16[72,2,256,256]{3,2,1,0:T(8,128)(2,1)}), bf16[72,2,256,256]{3,2,1,0:T(8,128)(2,1)}, u32[]{:S(2)}, u32[]{:S(2)}) async-start(bf16[72,2,256,256]{3,2,1,0:T(8,128)(2,1)} %gather_fusion.3), calls=%async_computation.6 | async-start | bytes 37748736 | tf_op jit(solution)/shard_map/all_to_all | solution.py:73
  849.3 38.8 %all-gather.3.cloned.1.call-start = ((), (), s32[]{:S(2)}) async-start(), calls=%async_computation.10 | async-start | bytes 5242880 | tf_op jit(solution)/shard_map/all_gather | solution.py:34
  850.6 421.8 %all-gather.5.cloned.1.call-start = ((), (), s32[]{:S(2)}) async-start(), calls=%async_computation.12 | async-start | bytes 5898240 | tf_op jit(solution)/shard_map/all_gather | solution.py:34
  851.8 441.0 %reduce-scatter.3.cloned.1.call-start = ((), (), s32[]{:S(2)}) async-start(), calls=%async_computation.11 | async-start | bytes 5242880 | tf_op jit(solution)/shard_map/reduce_scatter | solution.py:50
  888.1 6.1 copy-start.13
  888.1 11.7 slice-start
  894.2 6.3 slice-start.1
  903.9 436.8 %reduce-scatter.5.cloned.1.call-start = ((), (), s32[]{:S(2)}) async-start(), calls=%async_computation.13 | async-start | bytes 5898240 | tf_op jit(solution)/shard_map/reduce_scatter | solution.py:50
  1292.8 55.8 %copy-start.2 = (f32[48,8]{0,1:T(8,128)S(1)}, f32[48,8]{0,1:T(8,128)}, u32[]{:S(2)}) copy-start(f32[48,8]{0,1:T(8,128)} %param.22) | copy-start | bytes 4612
  1295.4 47.7 %all-to-all-start.1 = ((bf16[8,8,12,512]{3,1,2,0:T(8,128)(2,1)}), bf16[8,8,12,512]{3,1,2,0:T(8,128)(2,1)S(1)}, u32[]{:S(2)}, u32[]{:S(2)}) async-start(bf16[8,8,12,512]{3,1,2,0:T(8,128)(2,1)} %copy.106), calls=%async_computation.2 | async-start | bytes 1572864 | tf_op jit(solution)/shard_map/all_to_all | solution.py:53
  1299.8 57.7 %copy-start.14 = (s32[48]{0:T(128)S(1)}, s32[48]{0:T(128)}, u32[]{:S(2)}) copy-start(s32[48]{0:T(128)} %param.31) | copy-start | bytes 580
  1299.8 57.7 %copy-start.3 = (f32[48,8]{0,1:T(8,128)S(1)}, f32[48,8]{0,1:T(8,128)}, u32[]{:S(2)}) copy-start(f32[48,8]{0,1:T(8,128)} %param.18) | copy-start | bytes 4612
  1299.8 57.8 %copy-start.7 = (s32[384]{0:T(512)S(1)}, s32[384]{0:T(512)}, u32[]{:S(2)}) copy-start(s32[384]{0:T(512)} %copy-done.6) | copy-start | bytes 4612
  1299.8 57.9 %copy-start.5 = (s32[384]{0:T(512)S(1)}, s32[384]{0:T(512)}, u32[]{:S(2)}) copy-start(s32[384]{0:T(512)} %copy-done.4) | copy-start | bytes 4612
  1343.1 43.5 %all-to-all-start.7 = ((bf16[8,9,12,512]{3,2,1,0:T(8,128)(2,1)}), bf16[8,9,12,512]{3,2,1,0:T(8,128)(2,1)S(1)}, u32[]{:S(2)}, u32[]{:S(2)}) async-start(bf16[8,9,12,512]{3,2,1,0:T(8,128)(2,1)} %copy.121), calls=%async_computation.9 | async-start | bytes 2359296 | tf_op jit(solution)/shard_map/all_to_all | solution.py:53
  1370.1 19.1 %copy-start = (bf16[48,512]{1,0:T(8,128)(2,1)S(1)}, bf16[48,512]{1,0:T(8,128)(2,1)}, u32[]{:S(2)}) copy-start(bf16[48,512]{1,0:T(8,128)(2,1)} %param.20) | copy-start | bytes 147460
  1370.1 25.1 %copy-start.9 = (f32[512]{0:T(512)S(1)}, f32[512]{0:T(512)}, u32[]{:S(2)}) copy-start(f32[512]{0:T(512)} %param.27) | copy-start | bytes 6148
  1386.6 19.9 %copy-start.11 = (f32[128]{0:T(128)S(1)}, f32[128]{0:T(128)}, u32[]{:S(2)}) copy-start(f32[128]{0:T(128)} %param.30) | copy-start | bytes 1540
  1386.6 20.0 %copy-start.12 = (f32[128]{0:T(128)S(1)}, f32[128]{0:T(128)}, u32[]{:S(2)}) copy-start(f32[128]{0:T(128)} %param.29) | copy-start | bytes 1540
Sparse Core Ops, SparseCore 0:
  852.3 35.7 all-gather.2
  889.7 37.4 all-gather.4
  929.7 44.4 reduce-scatter.2
  1292.9 47.6 reduce-scatter.4
where the time goes:
time: 1430 us; the launch traced here: 1420 us
  waiting for transfers between devices  1100 us (77%)
  local copies, waits for them, and re-layouts  194 us (14%)
  starting transfers between devices  43 us (3%)
  matrix products  40.1 us (3%)
  between operations  14.8 us (1%)
    all_to_all x1, waiting for transfers between devices, migrate_first(): lax.all_to_all(gate_up, 'ep', split_axis=2, concat_axis=0, tiled=True)  339 us
    all_to_all x1, waiting for transfers between devices, migrate_second(): lax.all_to_all(table_gate_up[source], 'ep', split_axis=0, concat_axis=2,...  323 us
    all_to_all x1, waiting for transfers between devices, migrate_second(): lax.all_to_all(table_down[source], 'ep', split_axis=0, concat_axis=2, til...  175 us
    all_to_all x1, waiting for transfers between devices, migrate_first(): lax.all_to_all(down_proj, 'ep', split_axis=2, concat_axis=0, tiled=True)  165 us
    unnamed x41, local copies, waits for them, and re-layouts  58.8 us
    reduce_scatter x2, waiting for transfers between devices, run_batch(): lax.psum_scatter(partial_value.astype(jnp.bfloat16), 'tp', scatter_dimens...  40.8 us
    all_to_all x3, local copies, waits for them, and re-layouts, migrate_second(): lax.all_to_all(table_down[source], 'ep', split_axis=0, concat_axis=2, til...  37.1 us
    all_gather x2, waiting for transfers between devices, run_batch(): lax.all_gather(lax.all_to_all(outgoing, 'ep', split_axis=0, concat_axis=0...  36.2 us
  transfers between devices with their start and end apart: 12, of which 8 were waited for; matrix products, arithmetic and copies ran while one was open for 15% of the time, Pallas kernels for 0%

commit v1 on v0

--- a/solution.py
+++ b/solution.py
@@ -3,58 +3,87 @@
 import jax
 import jax.numpy as jnp
 from jax import lax
+from jax.experimental import pallas as pl
+from jax.experimental.pallas import tpu as pltpu
 from jax.sharding import PartitionSpec as P
 
 D = 2048
 EXPERTS = 64
 HEAD_DIM = 128
-CAP = 12
-
-
-def place_rows(routes, target_slot, total_slots):
-    flattened = routes.reshape(-1)
-    experts_range = jnp.arange(target_slot.shape[0], dtype=jnp.int32)
-    onehot = (flattened[:, None] == experts_range[None, :]).astype(jnp.int32)
-    position = jnp.sum((jnp.cumsum(onehot, axis=0) - 1) * onehot, axis=1)
-    slot_index = jnp.sum(onehot * target_slot[None, :], axis=1)
-    row_index = slot_index * CAP + position
-    owners = jnp.full((total_slots * CAP,), routes.shape[0], jnp.int32)
-    owners = owners.at[row_index].set(
-        jnp.arange(flattened.shape[0], dtype=jnp.int32) // routes.shape[1]
-    )
-    return (row_index, owners)
-
-
-def run_batch(tokens, routes, weights, target_slot, slot_gate_up, slot_down):
+
+
+def expert_body(x_ref, share_ref, gate_up_ref, down_ref, out_ref, total):
+    slot = pl.program_id(1)
+
+    @pl.when(slot == 0)
+    def _():
+        total[...] = jnp.zeros_like(total)
+
+    rows = 256 if x_ref.shape[0] % 256 == 0 else 48
+
+    def step(i, carry):
+        at = pl.ds(pl.multiple_of(i * rows, rows), rows)
+        x = x_ref[at, :]
+        gate_part = jnp.dot(x, gate_up_ref[0, 0], preferred_element_type=jnp.float32)
+        up_part = jnp.dot(x, gate_up_ref[0, 1], preferred_element_type=jnp.float32)
+        hidden = gate_part / (1.0 + jnp.exp(-gate_part)) * up_part * share_ref[0, at, :]
+        total[at, :] += jnp.dot(
+            hidden.astype(jnp.bfloat16), down_ref[0], preferred_element_type=jnp.float32
+        )
+        return carry
+
+    lax.fori_loop(0, x_ref.shape[0] // rows, step, 0)
+
+    @pl.when(slot == pl.num_programs(1) - 1)
+    def _():
+        out_ref[...] = total[...].astype(jnp.bfloat16)
+
+
+def expert_sums(x, shares, gate_up, down_proj):
+    count, width = x.shape
+    slots, _, _, units = gate_up.shape
+    block = 768 if count % 768 == 0 else count
+    return pl.pallas_call(
+        expert_body,
+        grid=(count // block, slots),
+        in_specs=[
+            pl.BlockSpec((block, width), lambda i, s: (i, 0)),
+            pl.BlockSpec((1, block, 1), lambda i, s: (s, i, 0)),
+            pl.BlockSpec((1, 2, width, units), lambda i, s: (s, 0, 0, 0)),
+            pl.BlockSpec((1, units, width), lambda i, s: (s, 0, 0)),
+        ],
+        out_specs=pl.BlockSpec((block, width), lambda i, s: (i, 0)),
+        out_shape=jax.ShapeDtypeStruct((count, width), jnp.bfloat16),
+        scratch_shapes=[pltpu.VMEM((block, width), jnp.float32)],
+        compiler_params=pltpu.CompilerParams(vmem_limit_bytes=48 * 1024 * 1024),
+        cost_estimate=pl.CostEstimate(
+            flops=6 * count * width * units * slots,
+            bytes_accessed=4 * count * width + 6 * slots * width * units,
+            transcendentals=count * units * slots,
+        ),
+    )(x, shares, gate_up, down_proj)
+
+
+def run_batches(tokens, routes, weights, old_place, gate_up, down_proj):
     ep_count = lax.axis_size("ep")
-    slots_here = slot_gate_up.shape[0]
-    row_index, owners = place_rows(routes, target_slot, ep_count * slots_here)
-    padded = jnp.concatenate([tokens, jnp.zeros((1, tokens.shape[1]), jnp.bfloat16)], axis=0)
-    outgoing = padded[owners].reshape(ep_count, slots_here, CAP, tokens.shape[1])
+    here = tokens.shape[0]
+    slots_here = gate_up.shape[0]
+    shares = weights / jnp.sum(weights, axis=1, keepdims=True)
+    all_shares = lax.all_gather(shares, "ep", axis=0, tiled=True)
+    all_routes = lax.all_gather(routes, "ep", axis=0, tiled=True)
     features = lax.all_gather(
-        lax.all_to_all(outgoing, "ep", split_axis=0, concat_axis=0, tiled=True),
-        "tp",
-        axis=3,
-        tiled=True,
-    )
-    gate_part = jnp.einsum(
-        "secd,edf->secf", features, slot_gate_up[:, 0], preferred_element_type=jnp.float32
-    )
-    up_part = jnp.einsum(
-        "secd,edf->secf", features, slot_gate_up[:, 1], preferred_element_type=jnp.float32
-    )
-    hidden = (jax.nn.silu(gate_part) * up_part).astype(jnp.bfloat16)
-    partial_value = jnp.einsum(
-        "secf,efd->secd", hidden, slot_down, preferred_element_type=jnp.float32
-    )
-    result = lax.psum_scatter(
-        partial_value.astype(jnp.bfloat16), "tp", scatter_dimension=3, tiled=True
-    )
-    returned = lax.all_to_all(result, "ep", split_axis=0, concat_axis=0, tiled=True)
-    flat_back = returned.reshape(-1, returned.shape[3])
-    picked = flat_back[row_index].astype(jnp.float32).reshape(routes.shape[0], routes.shape[1], -1)
-    shares = weights / jnp.sum(weights, axis=1, keepdims=True)
-    return jnp.sum(picked * shares[:, :, None], axis=1)
+        lax.all_gather(tokens, "ep", axis=0, tiled=True), "tp", axis=1, tiled=True
+    )
+    experts = lax.dynamic_slice_in_dim(old_place, lax.axis_index("ep") * slots_here, slots_here)
+    slot_shares = jnp.sum(
+        jnp.where(all_routes[None] == experts[:, None, None], all_shares[None], 0.0), axis=2
+    )
+    sums = expert_sums(features, slot_shares[:, :, None], gate_up, down_proj)
+    result = lax.psum_scatter(sums, "tp", scatter_dimension=1, tiled=True)
+    returned = lax.all_to_all(
+        result.reshape(ep_count, here, -1), "ep", split_axis=0, concat_axis=0, tiled=True
+    )
+    return jnp.sum(returned.astype(jnp.float32), axis=0)
 
 
 def migrate_first(gate_up, down_proj):
@@ -114,19 +143,20 @@
     experts_range = jnp.arange(EXPERTS, dtype=jnp.int32)
     old_slot = jnp.zeros((EXPERTS,), jnp.int32).at[old_place].set(experts_range)
     table_gate_up, table_down = migrate_first(gate_up, down_proj)
+    count = tokens_first.shape[0]
+    tokens = jnp.concatenate([tokens_first, tokens_second], axis=0)
+    tokens, table_down = lax.optimization_barrier((tokens, table_down))
+    mixed = run_batches(
+        tokens,
+        jnp.concatenate([routes_first, routes_second], axis=0),
+        jnp.concatenate([weights_first, weights_second], axis=0),
+        old_place,
+        gate_up,
+        down_proj,
+    )
     new_gate_up, new_down = migrate_second(table_gate_up, table_down, new_place, old_slot)
-    mixed_first = run_batch(tokens_first, routes_first, weights_first, old_slot, gate_up, down_proj)
-    output_first = mixed_first.astype(jnp.bfloat16)
-    slot_count = new_place.shape[0]
-    members = (new_place[:, None] == experts_range[None, :]).astype(jnp.int32)
-    replica_rank = jnp.cumsum(members, axis=0) - 1
-    replicas = jnp.sum(members, axis=0)
-    wanted = lax.axis_index("ep") % replicas
-    chosen = members * (replica_rank == wanted[None, :]).astype(jnp.int32)
-    new_target = jnp.sum(chosen * jnp.arange(slot_count, dtype=jnp.int32)[:, None], axis=0)
-    mixed_second = run_batch(
-        tokens_second, routes_second, weights_second, new_target, new_gate_up, new_down
-    )
+    output_first = mixed[:count].astype(jnp.bfloat16)
+    mixed_second = mixed[count:]
     stream = stream_second.astype(jnp.float32) + mixed_second
     squares = lax.psum(jnp.sum(stream * stream, axis=1), "tp")
     normed = (stream * lax.rsqrt(squares / D + 1e-06)[:, None] * attn_gain[None, :]).astype(

time: 1430 us -> 1430 us (level)
  blocking collectives: 11.5 us -> 107 us
  local copies, waits for them, and re-layouts: 194 us -> 138 us
  matrix products: 40.1 us -> 4.78 us
  Pallas kernels: 0 us -> 32.5 us
    all_gather x0 -> x3, blocking collectives: none -> 95.2 us  [the longest x1 34.4 us: run_batches(): lax.all_gather(tokens, 'ep', axis=0, tiled=True)]
    all_gather x2 -> x1, waiting for transfers between devices: 36.2 us -> 0.01 us  [run_batches(): lax.all_gather(lax.all_gather(tokens, 'ep', axis=0, tiled=True), 'tp', ax...]
    dot_general x6 -> x0, matrix products: 35.3 us -> none  [the longest x2 12.5 us: run_batch(): jnp.einsum('secd,edf->secf', features, slot_gate_up[:, 0], preferred_elem...]
    pallas_call x0 -> x1, Pallas kernels: none -> 32.5 us  [expert_sums(): pl.pallas_call(expert_body, grid=(count // block, slots), in_specs=[pl.Bl...]
    all_to_all x1, waiting for transfers between devices: 323 us -> 352 us  [migrate_second(): lax.all_to_all(table_gate_up[source], 'ep', split_axis=0, concat_axis=2,...]
    all_to_all x3 -> x1, local copies, waits for them, and re-layouts: 37.1 us -> 12.6 us  [migrate_second(): lax.all_to_all(table_down[source], 'ep', split_axis=0, concat_axis=2, til...]
    all_to_all x4 -> x1, waiting for transfers between devices: 25.6 us -> 2.31 us  [run_batches(): lax.all_to_all(result.reshape(ep_count, here, -1), 'ep', split_axis=0, co...]
    all_to_all x1, waiting for transfers between devices: 165 us -> 183 us  [migrate_first(): lax.all_to_all(down_proj, 'ep', split_axis=2, concat_axis=0, tiled=True)]
  transfers between devices with their start and end apart: 12 -> 7, of which waited for: 8 -> 6; matrix products, arithmetic and copies ran while one was open for 15% -> 7% of each run, Pallas kernels for 0% -> 0%
where the time goes in v1:
time: 1430 us
  waiting for transfers between devices  1100 us (77%)
  local copies, waits for them, and re-layouts  138 us (10%)
  blocking collectives  107 us (7%)
  Pallas kernels  32.5 us (2%)
  starting transfers between devices  29.7 us (2%)
  between operations  14.3 us (1%)
    all_to_all x1, waiting for transfers between devices, migrate_second(): lax.all_to_all(table_gate_up[source], 'ep', split_axis=0, concat_axis=2,...  352 us
    all_to_all x1, waiting for transfers between devices, migrate_first(): lax.all_to_all(gate_up, 'ep', split_axis=2, concat_axis=0, tiled=True)  351 us
    all_to_all x1, waiting for transfers between devices, migrate_first(): lax.all_to_all(down_proj, 'ep', split_axis=2, concat_axis=0, tiled=True)  183 us
    all_to_all x1, waiting for transfers between devices, migrate_second(): lax.all_to_all(table_down[source], 'ep', split_axis=0, concat_axis=2, til...  174 us
    unnamed x33, local copies, waits for them, and re-layouts  53 us
    reduce_scatter x1, waiting for transfers between devices, run_batches(): result = lax.psum_scatter(sums, 'tp', scatter_dimension=1, tiled=True)  36.9 us
    all_gather x1, blocking collectives, run_batches(): lax.all_gather(tokens, 'ep', axis=0, tiled=True)  34.4 us
    pallas_call x1, Pallas kernels, expert_sums(): pl.pallas_call(expert_body, grid=(count // block, slots), in_specs=[pl.Bl...  32.5 us
  transfers between devices with their start and end apart: 7, of which 6 were waited for; matrix products, arithmetic and copies ran while one was open for 7% of the time, Pallas kernels for 0%

profile of v1, /device:TPU:0, one launch (start us, length us, event | category | flops | bytes accessed | tf_op | source)
XLA Modules:
  0.0 1428.8 jit_solution(8813457211197826310)
XLA Ops:
  7.2 12.9 copy.82
  20.0 7.4 all-to-all-start
  27.6 183.0 %all-to-all-done = bf16[8,256,2048]{1,0,2:T(8,128)(2,1)} async-done(((bf16[8,256,2048]{1,0,2:T(8,128)(2,1)}), bf16[8,256,2048]{1,0,2:T(8,128)(2,1)}, u32[]{:S(2)}, u32[]{:S(2)}) %all-to-all-start) | async-done | bytes 8388640 | tf_op jit(solution)/shard_map/all_to_all | solution.py:92
  210.6 12.7 copy.84
  223.3 34.4 %all_gather.15 = bf16[768,512]{1,0:T(8,128)(2,1)} all-gather(bf16[96,512]{1,0:T(8,128)(2,1)S(1)} %pad_maximum_fusion), channel_id=1, replica_groups=mesh['ep'=8,'tp'=4] {'ep'}, dimensions={0}, use_global_device_ids=true | all-gather | bytes 884736 | tf_op jit(solution)/shard_map/all_gather | solution.py:75
  257.8 0.1 fusion.2
  257.9 0.1 divide_bitcast_fusion
  258.0 30.4 %all-gather.1 = f32[8,96,8]{1,2,0:T(8,128)S(1)} all-gather(f32[1,96,8]{1,2,0:T(8,128)S(1)} %divide_bitcast_fusion), channel_id=1, replica_groups=mesh['ep'=8,'tp'=4] {'ep'}, dimensions={0}, use_global_device_ids=true | all-gather | bytes 27648 | tf_op jit(solution)/shard_map/all_gather | solution.py:72
  288.4 0.1 reshape.144
  288.5 0.1 add_bitcast_fusion
  288.6 30.4 %all-gather = s32[8,96,8]{1,2,0:T(8,128)S(1)} all-gather(s32[1,96,8]{1,2,0:T(8,128)S(1)} %add_bitcast_fusion), channel_id=1, replica_groups=mesh['ep'=8,'tp'=4] {'ep'}, dimensions={0}, use_global_device_ids=true | all-gather | bytes 27648 | tf_op jit(solution)/shard_map/all_gather | solution.py:73
  319.0 0.1 reshape.142
  319.1 0.1 select_reduce_fusion
  319.3 2.2 copy.87.share_ref
  321.5 32.5 %shard_map.199 = bf16[768,2048]{1,0:T(8,128)(2,1)} custom-call(bf16[768,2048]{1,0:T(8,128)(2,1)} %all-gather.4.cloned.1.call-done.x_ref, f32[8,768,1]{2,1,0:T(8,128)} %copy.87.share_ref, bf16[8,2,2048,256]{3,2,1,0:T(8,128)(2,1)} %gate_up_ref.1, bf16[8,256,2048]{2,1,0:T(8,128)(2,1)} %down_ref.1), custom_call_target="tpu_custom_call" | custom-call | flops 19327352832 | bytes 31457280 | tf_op jit(solution)/shard_map/pallas_call | solution.py:46
  353.9 36.9 %reduce-scatter.2.cloned.1.call-done = bf16[768,512]{1,0:T(8,128)(2,1)} async-done(((bf16[768,2048]{1,0:T(8,128)(2,1)}), bf16[768,512]{1,0:T(8,128)(2,1)}) %reduce-scatter.2.cloned.1.call-update) | async-done | bytes 786448 | tf_op jit(solution)/shard_map/reduce_scatter | solution.py:82
  390.8 5.5 all-to-all-start.1
  396.3 17.9 %copy.92 = bf16[8,2,2048,256]{3,0,1,2:T(8,128)(2,1)} copy(bf16[8,2,2048,256]{3,2,1,0:T(8,128)(2,1)} %gate_up_ref.1) | data formatting | bytes 33554432 | tf_op args[9]
  414.2 2.3 all-to-all-done.1
  416.5 5.7 all-to-all-start.2
  422.3 0.8 scatter_custom_fusion
  423.1 0.1 select_reduce_fusion.1
  423.2 9.3 gather_fusion.1
  432.5 351.5 %all-to-all-done.2 = bf16[8,2,2048,256]{3,0,1,2:T(8,128)(2,1)} async-done(((bf16[8,2,2048,256]{3,0,1,2:T(8,128)(2,1)}), bf16[8,2,2048,256]{3,0,1,2:T(8,128)(2,1)}, u32[]{:S(2)}, u32[]{:S(2)}) %all-to-all-start.2) | async-done | bytes 16777248 | tf_op jit(solution)/shard_map/all_to_all | solution.py:91
  784.0 5.1 all-to-all-start.4
  789.0 16.0 %copy.94 = bf16[8,8,2,256,256]{4,3,2,1,0:T(8,128)(2,1)} copy(bf16[8,8,2,256,256]{4,1,2,3,0:T(8,128)(2,1)} %bitcast.17) | data formatting | bytes 33554432 | tf_op jit(solution)/shard_map/all_to_all | solution.py:91
  805.0 14.2 gather_fusion
  819.2 174.1 %all-to-all-done.4 = bf16[72,256,256]{2,1,0:T(8,128)(2,1)} async-done(((bf16[72,256,256]{2,1,0:T(8,128)(2,1)}), bf16[72,256,256]{2,1,0:T(8,128)(2,1)}, u32[]{:S(2)}, u32[]{:S(2)}) %all-to-all-start.4) | async-done | bytes 9437216 | tf_op jit(solution)/shard_map/all_to_all | solution.py:103
  993.3 5.9 all-to-all-start.3
  999.3 8.8 copy.88
  1008.1 0.2 multiply_cosine_fusion
  1008.3 0.1 convert_reduce_fusion
  1008.4 0.6 slice.77
  1009.0 0.1 multiply_reduce_fusion.2
  1009.2 6.1 psum.7
  1015.2 0.1 multiply_convert_fusion
  1015.3 5.8 all_gather.19
  1021.1 4.8 fusion
  1026.0 0.6 copy.107
  1026.6 0.1 multiply_reduce_fusion
  1026.8 0.1 multiply_multiply_fusion
  1026.9 0.1 subtract_convert_fusion
  1027.0 0.7 copy_bitcast_fusion.2
  1027.7 0.7 copy_bitcast_fusion.1
  1028.4 12.6 copy.96
  1041.0 12.6 copy.97
  1053.7 351.6 %all-to-all-done.3 = bf16[72,2,256,256]{3,2,1,0:T(8,128)(2,1)} async-done(((bf16[72,2,256,256]{3,2,1,0:T(8,128)(2,1)}), bf16[72,2,256,256]{3,2,1,0:T(8,128)(2,1)}, u32[]{:S(2)}, u32[]{:S(2)}) %all-to-all-start.3) | async-done | bytes 18874400 | tf_op jit(solution)/shard_map/all_to_all | solution.py:102
  1405.3 16.7 %copy.95 = bf16[9,2,8,256,256]{4,3,2,1,0:T(8,128)(2,1)} copy(bf16[9,2,8,256,256]{4,3,1,0,2:T(8,128)(2,1)} %bitcast.22) | data formatting | bytes 37748736 | tf_op jit(solution)/shard_map/all_to_all | solution.py:102
  (45 shorter events, 0.4 us)
Async XLA Ops:
  20.0 7.5 copy-start.1
  20.0 7.5 copy-start.2
  20.0 190.6 %all-to-all-start = ((bf16[8,256,2048]{1,0,2:T(8,128)(2,1)}), bf16[8,256,2048]{1,0,2:T(8,128)(2,1)}, u32[]{:S(2)}, u32[]{:S(2)}) async-start(bf16[8,256,2048]{1,0,2:T(8,128)(2,1)} %copy.82), calls=%async_computation | async-start | bytes 16777216 | tf_op jit(solution)/shard_map/all_to_all | solution.py:92
  27.4 230.4 %copy-start.3 = (f32[48,8]{0,1:T(8,128)S(1)}, f32[48,8]{0,1:T(8,128)}, u32[]{:S(2)}) copy-start(f32[48,8]{0,1:T(8,128)} %param.22) | copy-start | bytes 4612
  27.4 230.4 %copy-start.4 = (f32[48,8]{0,1:T(8,128)S(1)}, f32[48,8]{0,1:T(8,128)}, u32[]{:S(2)}) copy-start(f32[48,8]{0,1:T(8,128)} %param.18) | copy-start | bytes 4612
  27.5 261.0 %copy-start.5 = (s32[48,8]{0,1:T(8,128)S(1)}, s32[48,8]{0,1:T(8,128)}, u32[]{:S(2)}) copy-start(s32[48,8]{0,1:T(8,128)} %param.21) | copy-start | bytes 4612
  27.5 261.0 %copy-start.6 = (s32[48,8]{0,1:T(8,128)S(1)}, s32[48,8]{0,1:T(8,128)}, u32[]{:S(2)}) copy-start(s32[48,8]{0,1:T(8,128)} %param.17) | copy-start | bytes 4612
  27.5 294.0 %all-gather.4.cloned.1.call-start = ((), (), s32[]{:S(2)}) async-start(), calls=%async_computation.6 | async-start | bytes 3932160 | tf_op jit(solution)/shard_map/all_gather | solution.py:74
  27.6 291.5 %copy-start.10 = (s32[64]{0:T(128)S(1)}, s32[64]{0:T(128)}, u32[]{:S(2)}) copy-start(s32[64]{0:T(128)} %param.23) | copy-start | bytes 772
  257.7 133.0 %reduce-scatter.2.cloned.1.call-start = ((), (), s32[]{:S(2)}) async-start(), calls=%async_computation.7 | async-start | bytes 3932160 | tf_op jit(solution)/shard_map/reduce_scatter | solution.py:82
  390.8 25.7 %all-to-all-start.1 = ((bf16[8,96,512]{2,1,0:T(8,128)(2,1)}), bf16[8,96,512]{2,1,0:T(8,128)(2,1)S(1)}, u32[]{:S(2)}, u32[]{:S(2)}) async-start(bf16[8,96,512]{2,1,0:T(8,128)(2,1)} %bitcast.74), calls=%async_computation.2 | async-start | bytes 1572864 | tf_op jit(solution)/shard_map/all_to_all | solution.py:83
  414.2 8.9 copy-start.11
  416.5 367.5 %all-to-all-start.2 = ((bf16[8,2,2048,256]{3,0,1,2:T(8,128)(2,1)}), bf16[8,2,2048,256]{3,0,1,2:T(8,128)(2,1)}, u32[]{:S(2)}, u32[]{:S(2)}) async-start(bf16[8,2,2048,256]{3,0,1,2:T(8,128)(2,1)} %copy.92), calls=%async_computation.3 | async-start | bytes 33554432 | tf_op jit(solution)/shard_map/all_to_all | solution.py:91
  784.0 209.4 %all-to-all-start.4 = ((bf16[72,256,256]{2,1,0:T(8,128)(2,1)}), bf16[72,256,256]{2,1,0:T(8,128)(2,1)}, u32[]{:S(2)}, u32[]{:S(2)}) async-start(bf16[72,256,256]{2,1,0:T(8,128)(2,1)} %gather_fusion.1), calls=%async_computation.5 | async-start | bytes 18874368 | tf_op jit(solution)/shard_map/all_to_all | solution.py:103
  993.3 412.0 %all-to-all-start.3 = ((bf16[72,2,256,256]{3,2,1,0:T(8,128)(2,1)}), bf16[72,2,256,256]{3,2,1,0:T(8,128)(2,1)}, u32[]{:S(2)}, u32[]{:S(2)}) async-start(bf16[72,2,256,256]{3,2,1,0:T(8,128)(2,1)} %gather_fusion), calls=%async_computation.4 | async-start | bytes 37748736 | tf_op jit(solution)/shard_map/all_to_all | solution.py:102
  999.3 8.8 copy-start.12
  999.3 9.8 copy-start
  999.3 16.0 %copy-start.7 = (f32[512]{0:T(512)S(1)}, f32[512]{0:T(512)}, u32[]{:S(2)}) copy-start(f32[512]{0:T(512)} %param.27) | copy-start | bytes 6148
  999.3 27.4 %copy-start.8 = (f32[128]{0:T(128)S(1)}, f32[128]{0:T(128)}, u32[]{:S(2)}) copy-start(f32[128]{0:T(128)} %param.30) | copy-start | bytes 1540
  999.3 27.4 %copy-start.9 = (f32[128]{0:T(128)S(1)}, f32[128]{0:T(128)}, u32[]{:S(2)}) copy-start(f32[128]{0:T(128)} %param.29) | copy-start | bytes 1540
Sparse Core Ops, SparseCore 0:
  257.9 27.2 all-gather.3
  354.1 36.6 reduce-scatter.1

commit v2 on v1

--- a/solution.py
+++ b/solution.py
@@ -65,12 +65,13 @@
 
 
 def run_batches(tokens, routes, weights, old_place, gate_up, down_proj):
-    ep_count = lax.axis_size("ep")
-    here = tokens.shape[0]
     slots_here = gate_up.shape[0]
     shares = weights / jnp.sum(weights, axis=1, keepdims=True)
-    all_shares = lax.all_gather(shares, "ep", axis=0, tiled=True)
-    all_routes = lax.all_gather(routes, "ep", axis=0, tiled=True)
+    choices = lax.all_gather(
+        jnp.concatenate([shares, routes.astype(jnp.float32)], axis=1), "ep", axis=0, tiled=True
+    )
+    all_shares = choices[:, : shares.shape[1]]
+    all_routes = choices[:, shares.shape[1] :].astype(jnp.int32)
     features = lax.all_gather(
         lax.all_gather(tokens, "ep", axis=0, tiled=True), "tp", axis=1, tiled=True
     )
@@ -80,10 +81,7 @@
     )
     sums = expert_sums(features, slot_shares[:, :, None], gate_up, down_proj)
     result = lax.psum_scatter(sums, "tp", scatter_dimension=1, tiled=True)
-    returned = lax.all_to_all(
-        result.reshape(ep_count, here, -1), "ep", split_axis=0, concat_axis=0, tiled=True
-    )
-    return jnp.sum(returned.astype(jnp.float32), axis=0)
+    return lax.psum_scatter(result, "ep", scatter_dimension=0, tiled=True).astype(jnp.float32)
 
 
 def migrate_first(gate_up, down_proj):

time: 1430 us -> 1470 us (1.028)
  blocking collectives: 107 us -> 472 us
  waiting for transfers between devices: 1100 us -> 774 us
    all_gather x1, blocking collectives: 34.4 us -> 430 us  [run_batches(): lax.all_gather(tokens, 'ep', axis=0, tiled=True)]
    all_to_all x1, waiting for transfers between devices: 352 us -> 0.01 us  [migrate_second(): lax.all_to_all(table_gate_up[source], 'ep', split_axis=0, concat_axis=2,...]
    reduce_scatter x0 -> x1, waiting for transfers between devices: none -> 57.1 us  [run_batches(): lax.psum_scatter(result, 'ep', scatter_dimension=0, tiled=True)]
    all_gather x2 -> x1, blocking collectives: 60.8 us -> 30.5 us  [run_batches(): lax.all_gather(jnp.concatenate([shares, routes.astype(jnp.float32)], axis...]
    all_to_all x1, waiting for transfers between devices: 183 us -> 165 us  [migrate_first(): lax.all_to_all(down_proj, 'ep', split_axis=2, concat_axis=0, tiled=True)]
    unnamed x33 -> x32, local copies, waits for them, and re-layouts: 53 us -> 52.9 us
  transfers between devices with their start and end apart: 7 -> 7, of which waited for: 6 -> 5; matrix products, arithmetic and copies ran while one was open for 7% -> 8% of each run, Pallas kernels for 0% -> 2%
where the time goes in v2:
time: 1470 us; the launch traced here: 1460 us
  waiting for transfers between devices  774 us (53%)
  blocking collectives  472 us (32%)
  local copies, waits for them, and re-layouts  139 us (9%)
  Pallas kernels  32.5 us (2%)
  starting transfers between devices  24.1 us (2%)
    all_gather x1, blocking collectives, run_batches(): lax.all_gather(tokens, 'ep', axis=0, tiled=True)  430 us
    all_to_all x1, waiting for transfers between devices, migrate_first(): lax.all_to_all(gate_up, 'ep', split_axis=2, concat_axis=0, tiled=True)  339 us
    all_to_all x1, waiting for transfers between devices, migrate_second(): lax.all_to_all(table_down[source], 'ep', split_axis=0, concat_axis=2, til...  174 us
    all_to_all x1, waiting for transfers between devices, migrate_first(): lax.all_to_all(down_proj, 'ep', split_axis=2, concat_axis=0, tiled=True)  165 us
    reduce_scatter x1, waiting for transfers between devices, run_batches(): lax.psum_scatter(result, 'ep', scatter_dimension=0, tiled=True)  57.1 us
    unnamed x32, local copies, waits for them, and re-layouts  52.9 us
    reduce_scatter x1, waiting for transfers between devices, run_batches(): result = lax.psum_scatter(sums, 'tp', scatter_dimension=1, tiled=True)  38.2 us
    pallas_call x1, Pallas kernels, expert_sums(): pl.pallas_call(expert_body, grid=(count // block, slots), in_specs=[pl.Bl...  32.5 us
  transfers between devices with their start and end apart: 7, of which 5 were waited for; matrix products, arithmetic and copies ran while one was open for 8% of the time, Pallas kernels for 2%

profile of v2, /device:TPU:0, one launch (start us, length us, event | category | flops | bytes accessed | tf_op | source)
XLA Modules:
  0.0 1464.4 jit_solution(12121201934971770290)
XLA Ops:
  7.2 12.9 copy.78
  20.0 7.3 all-to-all-start
  27.3 17.9 %copy.87 = bf16[8,2,2048,256]{3,0,1,2:T(8,128)(2,1)} copy(bf16[8,2,2048,256]{3,2,1,0:T(8,128)(2,1)} %gate_up_ref.1) | data formatting | bytes 33554432 | tf_op args[9]
  45.2 165.3 %all-to-all-done = bf16[8,256,2048]{1,0,2:T(8,128)(2,1)} async-done(((bf16[8,256,2048]{1,0,2:T(8,128)(2,1)}), bf16[8,256,2048]{1,0,2:T(8,128)(2,1)}, u32[]{:S(2)}, u32[]{:S(2)}) %all-to-all-start) | async-done | bytes 8388640 | tf_op jit(solution)/shard_map/all_to_all | solution.py:90
  210.5 5.8 all-to-all-start.1
  216.3 0.8 scatter_custom_fusion
  217.1 0.1 select_reduce_fusion.1
  217.2 12.7 copy.80
  229.9 9.3 gather_fusion.1
  239.2 339.0 %all-to-all-done.1 = bf16[8,2,2048,256]{3,0,1,2:T(8,128)(2,1)} async-done(((bf16[8,2,2048,256]{3,0,1,2:T(8,128)(2,1)}), bf16[8,2,2048,256]{3,0,1,2:T(8,128)(2,1)}, u32[]{:S(2)}, u32[]{:S(2)}) %all-to-all-start.1) | async-done | bytes 16777248 | tf_op jit(solution)/shard_map/all_to_all | solution.py:89
  578.2 5.1 all-to-all-start.3
  583.3 16.0 %copy.89 = bf16[8,8,2,256,256]{4,3,2,1,0:T(8,128)(2,1)} copy(bf16[8,8,2,256,256]{4,1,2,3,0:T(8,128)(2,1)} %bitcast.15) | data formatting | bytes 33554432 | tf_op jit(solution)/shard_map/all_to_all | solution.py:89
  599.2 14.2 gather_fusion
  613.4 174.2 %all-to-all-done.3 = bf16[72,256,256]{2,1,0:T(8,128)(2,1)} async-done(((bf16[72,256,256]{2,1,0:T(8,128)(2,1)}), bf16[72,256,256]{2,1,0:T(8,128)(2,1)}, u32[]{:S(2)}, u32[]{:S(2)}) %all-to-all-start.3) | async-done | bytes 9437216 | tf_op jit(solution)/shard_map/all_to_all | solution.py:101
  787.6 5.9 all-to-all-start.2
  793.5 0.0 all-gather.3.cloned.1.call-start
  793.5 430.1 %all_gather.12 = bf16[768,512]{1,0:T(8,128)(2,1)} all-gather(bf16[96,512]{1,0:T(8,128)(2,1)S(1)} %pad_maximum_fusion), channel_id=1, replica_groups=mesh['ep'=8,'tp'=4] {'ep'}, dimensions={0}, use_global_device_ids=true | all-gather | bytes 884736 | tf_op jit(solution)/shard_map/all_gather | solution.py:76
  1223.7 0.0 all-gather.3.cloned.1.call-update
  1223.7 0.0 reduce-scatter.3.cloned.1.call-start
  1223.8 0.1 fusion.2
  1223.9 0.1 add_convert_fusion.2
  1223.9 0.1 broadcast_divide_fusion
  1224.0 30.5 %all-gather = f32[8,96,16]{1,2,0:T(8,128)S(1)} all-gather(f32[1,96,16]{1,2,0:T(8,128)S(1)} %maximum_bitcast_fusion.2), channel_id=1, replica_groups=mesh['ep'=8,'tp'=4] {'ep'}, dimensions={0}, use_global_device_ids=true | all-gather | bytes 55296 | tf_op jit(solution)/shard_map/all_gather | solution.py:70
  1254.5 0.1 reshape.138
  1254.6 0.1 dynamic_slice.3
  1254.7 0.1 select_reduce_fusion
  1254.9 2.2 copy.82.share_ref
  1257.1 32.5 %shard_map.199 = bf16[768,2048]{1,0:T(8,128)(2,1)} custom-call(bf16[768,2048]{1,0:T(8,128)(2,1)} %all-gather.3.cloned.1.call-done.x_ref, f32[8,768,1]{2,1,0:T(8,128)} %copy.82.share_ref, bf16[8,2,2048,256]{3,2,1,0:T(8,128)(2,1)} %gate_up_ref.1, bf16[8,256,2048]{2,1,0:T(8,128)(2,1)} %down_ref.1), custom_call_target="tpu_custom_call" | custom-call | flops 19327352832 | bytes 31457280 | tf_op jit(solution)/shard_map/pallas_call | solution.py:46
  1289.5 0.0 reduce-scatter.5.cloned.1.call-start
  1289.6 38.2 %reduce-scatter.3.cloned.1.call-done = bf16[768,512]{1,0:T(8,128)(2,1)} async-done(((bf16[768,2048]{1,0:T(8,128)(2,1)}), bf16[768,512]{1,0:T(8,128)(2,1)}) %reduce-scatter.3.cloned.1.call-update) | async-done | bytes 786448 | tf_op jit(solution)/shard_map/reduce_scatter | solution.py:83
  1327.8 8.8 copy.83
  1336.6 0.2 multiply_cosine_fusion
  1336.8 57.1 %reduce-scatter.5.cloned.1.call-done = bf16[96,512]{1,0:T(8,128)(2,1)} async-done(((bf16[768,512]{1,0:T(8,128)(2,1)}), bf16[96,512]{1,0:T(8,128)(2,1)}) %reduce-scatter.5.cloned.1.call-update) | async-done | bytes 98320 | tf_op jit(solution)/shard_map/reduce_scatter | solution.py:84
  1393.9 0.9 multiply_reduce_fusion.2
  1394.8 5.7 psum.7
  1400.5 0.9 multiply_convert_fusion
  1401.4 5.8 all_gather.15
  1407.2 4.8 fusion
  1412.0 0.6 copy.102
  1412.6 1.4 slice.56
  1414.1 0.1 multiply_reduce_fusion
  1414.2 0.1 multiply_multiply_fusion
  1414.4 0.1 subtract_convert_fusion
  1414.5 0.7 copy_bitcast_fusion.2
  1415.2 0.7 copy_bitcast_fusion.1
  1415.9 12.7 copy.91
  1428.6 12.6 copy.92
  1441.2 16.7 %copy.90 = bf16[9,2,8,256,256]{4,3,2,1,0:T(8,128)(2,1)} copy(bf16[9,2,8,256,256]{4,3,1,0,2:T(8,128)(2,1)} %bitcast.20) | data formatting | bytes 37748736 | tf_op jit(solution)/shard_map/all_to_all | solution.py:100
  (44 shorter events, 0.2 us)
Async XLA Ops:
  20.0 190.4 %all-to-all-start = ((bf16[8,256,2048]{1,0,2:T(8,128)(2,1)}), bf16[8,256,2048]{1,0,2:T(8,128)(2,1)}, u32[]{:S(2)}, u32[]{:S(2)}) async-start(bf16[8,256,2048]{1,0,2:T(8,128)(2,1)} %copy.78), calls=%async_computation | async-start | bytes 16777216 | tf_op jit(solution)/shard_map/all_to_all | solution.py:90
  45.2 171.1 %copy-start.11 = (s32[64]{0:T(128)S(1)}, s32[64]{0:T(128)}, u32[]{:S(2)}) copy-start(s32[64]{0:T(128)} %param.23) | copy-start | bytes 772
  45.2 171.9 %copy-start.10 = (s32[72]{0:T(128)S(1)}, s32[72]{0:T(128)}, u32[]{:S(2)}) copy-start(s32[72]{0:T(128)} %param.24) | copy-start | bytes 868
  45.2 172.0 %copy-start.1 = (bf16[48,512]{1,0:T(8,128)(2,1)S(1)}, bf16[48,512]{1,0:T(8,128)(2,1)}, u32[]{:S(2)}) copy-start(bf16[48,512]{1,0:T(8,128)(2,1)} %param.19) | copy-start | bytes 147460
  45.2 172.0 %copy-start.2 = (bf16[48,512]{1,0:T(8,128)(2,1)S(1)}, bf16[48,512]{1,0:T(8,128)(2,1)}, u32[]{:S(2)}) copy-start(bf16[48,512]{1,0:T(8,128)(2,1)} %param.16) | copy-start | bytes 147460
  210.5 367.7 %all-to-all-start.1 = ((bf16[8,2,2048,256]{3,0,1,2:T(8,128)(2,1)}), bf16[8,2,2048,256]{3,0,1,2:T(8,128)(2,1)}, u32[]{:S(2)}, u32[]{:S(2)}) async-start(bf16[8,2,2048,256]{3,0,1,2:T(8,128)(2,1)} %copy.87), calls=%async_computation.3 | async-start | bytes 33554432 | tf_op jit(solution)/shard_map/all_to_all | solution.py:89
  578.2 209.4 %all-to-all-start.3 = ((bf16[72,256,256]{2,1,0:T(8,128)(2,1)}), bf16[72,256,256]{2,1,0:T(8,128)(2,1)}, u32[]{:S(2)}, u32[]{:S(2)}) async-start(bf16[72,256,256]{2,1,0:T(8,128)(2,1)} %gather_fusion.1), calls=%async_computation.5 | async-start | bytes 18874368 | tf_op jit(solution)/shard_map/all_to_all | solution.py:101
  613.4 610.3 %copy-start.3 = (f32[48,8]{0,1:T(8,128)S(1)}, f32[48,8]{0,1:T(8,128)}, u32[]{:S(2)}) copy-start(f32[48,8]{0,1:T(8,128)} %param.22) | copy-start | bytes 4612
  613.4 610.3 %copy-start.4 = (f32[48,8]{0,1:T(8,128)S(1)}, f32[48,8]{0,1:T(8,128)}, u32[]{:S(2)}) copy-start(f32[48,8]{0,1:T(8,128)} %param.18) | copy-start | bytes 4612
  613.4 610.4 %copy-start.5 = (s32[48,8]{0,1:T(8,128)S(1)}, s32[48,8]{0,1:T(8,128)}, u32[]{:S(2)}) copy-start(s32[48,8]{0,1:T(8,128)} %param.21) | copy-start | bytes 4612
  613.4 610.4 %copy-start.6 = (s32[48,8]{0,1:T(8,128)S(1)}, s32[48,8]{0,1:T(8,128)}, u32[]{:S(2)}) copy-start(s32[48,8]{0,1:T(8,128)} %param.17) | copy-start | bytes 4612
  787.6 653.6 %all-to-all-start.2 = ((bf16[72,2,256,256]{3,2,1,0:T(8,128)(2,1)}), bf16[72,2,256,256]{3,2,1,0:T(8,128)(2,1)}, u32[]{:S(2)}, u32[]{:S(2)}) async-start(bf16[72,2,256,256]{3,2,1,0:T(8,128)(2,1)} %gather_fusion), calls=%async_computation.4 | async-start | bytes 37748736 | tf_op jit(solution)/shard_map/all_to_all | solution.py:100
  793.5 463.6 %all-gather.3.cloned.1.call-start = ((), (), s32[]{:S(2)}) async-start(), calls=%async_computation.6 | async-start | bytes 3932160 | tf_op jit(solution)/shard_map/all_gather | solution.py:75
  1223.7 104.1 %reduce-scatter.3.cloned.1.call-start = ((), (), s32[]{:S(2)}) async-start(), calls=%async_computation.7 | async-start | bytes 3932160 | tf_op jit(solution)/shard_map/reduce_scatter | solution.py:83
  1289.5 47.1 %copy-start.12 = (s32[48]{0:T(128)S(1)}, s32[48]{0:T(128)}, u32[]{:S(2)}) copy-start(s32[48]{0:T(128)} %param.31) | copy-start | bytes 580
  1289.5 104.4 %copy-start = (bf16[48,512]{1,0:T(8,128)(2,1)S(1)}, bf16[48,512]{1,0:T(8,128)(2,1)}, u32[]{:S(2)}) copy-start(bf16[48,512]{1,0:T(8,128)(2,1)} %param.20) | copy-start | bytes 147460
  1289.5 111.0 %copy-start.7 = (f32[512]{0:T(512)S(1)}, f32[512]{0:T(512)}, u32[]{:S(2)}) copy-start(f32[512]{0:T(512)} %param.27) | copy-start | bytes 6148
  1289.5 104.3 %reduce-scatter.5.cloned.1.call-start = ((), (), s32[]{:S(2)}) async-start(), calls=%async_computation.8 | async-start | bytes 884736 | tf_op jit(solution)/shard_map/reduce_scatter | solution.py:84
  1327.8 86.4 %copy-start.8 = (f32[128]{0:T(128)S(1)}, f32[128]{0:T(128)}, u32[]{:S(2)}) copy-start(f32[128]{0:T(128)} %param.30) | copy-start | bytes 1540
  1327.8 86.4 %copy-start.9 = (f32[128]{0:T(128)S(1)}, f32[128]{0:T(128)}, u32[]{:S(2)}) copy-start(f32[128]{0:T(128)} %param.29) | copy-start | bytes 1540
Sparse Core Ops, SparseCore 0:
  1223.8 28.6 all-gather.2
  1289.7 38.0 reduce-scatter.2
  1331.4 62.4 reduce-scatter.4

commit v3 on v2

--- a/solution.py
+++ b/solution.py
@@ -64,42 +64,42 @@
     )(x, shares, gate_up, down_proj)
 
 
-def run_batches(tokens, routes, weights, old_place, gate_up, down_proj):
+def gather_rows(values):
+    count = lax.axis_size("ep")
+    spread = jnp.broadcast_to(values[None], (count,) + values.shape)
+    gathered = lax.all_to_all(spread, "ep", split_axis=0, concat_axis=0, tiled=True)
+    return gathered.reshape((count * values.shape[0],) + values.shape[1:])
+
+
+def expert_mixture(features, choices, old_place, gate_up, down_proj):
     slots_here = gate_up.shape[0]
-    shares = weights / jnp.sum(weights, axis=1, keepdims=True)
-    choices = lax.all_gather(
-        jnp.concatenate([shares, routes.astype(jnp.float32)], axis=1), "ep", axis=0, tiled=True
-    )
-    all_shares = choices[:, : shares.shape[1]]
-    all_routes = choices[:, shares.shape[1] :].astype(jnp.int32)
-    features = lax.all_gather(
-        lax.all_gather(tokens, "ep", axis=0, tiled=True), "tp", axis=1, tiled=True
-    )
+    top = choices.shape[1] // 2
+    all_shares = choices[:, :top]
+    all_routes = choices[:, top:].astype(jnp.int32)
     experts = lax.dynamic_slice_in_dim(old_place, lax.axis_index("ep") * slots_here, slots_here)
     slot_shares = jnp.sum(
         jnp.where(all_routes[None] == experts[:, None, None], all_shares[None], 0.0), axis=2
     )
+    features = lax.all_gather(features, "tp", axis=1, tiled=True)
     sums = expert_sums(features, slot_shares[:, :, None], gate_up, down_proj)
-    result = lax.psum_scatter(sums, "tp", scatter_dimension=1, tiled=True)
-    return lax.psum_scatter(result, "ep", scatter_dimension=0, tiled=True).astype(jnp.float32)
-
-
-def migrate_first(gate_up, down_proj):
-    return (
-        lax.all_to_all(gate_up, "ep", split_axis=2, concat_axis=0, tiled=True),
-        lax.all_to_all(down_proj, "ep", split_axis=2, concat_axis=0, tiled=True),
-    )
-
-
-def migrate_second(table_gate_up, table_down, new_place, old_slot):
+    return lax.psum_scatter(sums, "tp", scatter_dimension=1, tiled=True)
+
+
+def exchange(blocks):
+    return lax.all_to_all(blocks, "ep", split_axis=0, concat_axis=0, tiled=True)
+
+
+def by_destination(gate_up):
+    count = lax.axis_size("ep")
+    slots, pair, width, units = gate_up.shape
+    return gate_up.reshape(slots, pair, count, width // count, units).transpose(2, 0, 1, 3, 4)
+
+
+def slot_source(new_place, old_slot):
     members = (
         new_place[:, None] == jnp.arange(old_slot.shape[0], dtype=jnp.int32)[None, :]
     ).astype(jnp.int32)
-    source = jnp.sum(members * old_slot[None, :], axis=1)
-    return (
-        lax.all_to_all(table_gate_up[source], "ep", split_axis=0, concat_axis=2, tiled=True),
-        lax.all_to_all(table_down[source], "ep", split_axis=0, concat_axis=2, tiled=True),
-    )
+    return jnp.sum(members * old_slot[None, :], axis=1)
 
 
 def head_norm(values, gain):
@@ -140,19 +140,33 @@
 ):
     experts_range = jnp.arange(EXPERTS, dtype=jnp.int32)
     old_slot = jnp.zeros((EXPERTS,), jnp.int32).at[old_place].set(experts_range)
-    table_gate_up, table_down = migrate_first(gate_up, down_proj)
+    source = slot_source(new_place, old_slot)
+    ep_count = lax.axis_size("ep")
     count = tokens_first.shape[0]
     tokens = jnp.concatenate([tokens_first, tokens_second], axis=0)
-    tokens, table_down = lax.optimization_barrier((tokens, table_down))
-    mixed = run_batches(
-        tokens,
-        jnp.concatenate([routes_first, routes_second], axis=0),
-        jnp.concatenate([weights_first, weights_second], axis=0),
-        old_place,
-        gate_up,
-        down_proj,
-    )
-    new_gate_up, new_down = migrate_second(table_gate_up, table_down, new_place, old_slot)
+    routes = jnp.concatenate([routes_first, routes_second], axis=0)
+    weights = jnp.concatenate([weights_first, weights_second], axis=0)
+    shares = weights / jnp.sum(weights, axis=1, keepdims=True)
+    choices = gather_rows(jnp.concatenate([shares, routes.astype(jnp.float32)], axis=1))
+    features = gather_rows(tokens)
+
+    send_gate_up = by_destination(gate_up)
+    send_down, features, choices = lax.optimization_barrier((down_proj, features, choices))
+    table_down = lax.all_to_all(send_down, "ep", split_axis=2, concat_axis=0, tiled=True)
+    features, choices, table_down = lax.optimization_barrier((features, choices, table_down))
+    table_gate_up = exchange(send_gate_up)
+    sums = expert_mixture(features, choices, old_place, gate_up, down_proj)
+    sums, table_gate_up = lax.optimization_barrier((sums, table_gate_up))
+    returned = exchange(sums.reshape(ep_count, 2 * count, -1))
+    returned, table_gate_up = lax.optimization_barrier((returned, table_gate_up))
+    mixed = jnp.sum(returned.astype(jnp.float32), axis=0)
+    table_gate_up = table_gate_up.reshape((-1,) + table_gate_up.shape[2:])
+    back_down = exchange(table_down[source].reshape((ep_count, -1) + table_down.shape[1:]))
+    back_gate_up = exchange(
+        table_gate_up[source].reshape((ep_count, -1) + table_gate_up.shape[1:])
+    )
+    new_down = back_down.transpose(1, 2, 0, 3).reshape((-1,) + down_proj.shape[1:])
+    new_gate_up = back_gate_up.transpose(1, 2, 0, 3, 4).reshape((-1,) + gate_up.shape[1:])
     output_first = mixed[:count].astype(jnp.bfloat16)
     mixed_second = mixed[count:]
     stream = stream_second.astype(jnp.float32) + mixed_second

time: 1470 us -> 1290 us (0.88)
  blocking collectives: 472 us -> 11.7 us
  waiting for transfers between devices: 774 us -> 1060 us
  local copies, waits for them, and re-layouts: 139 us -> 120 us
    all_gather x2 -> x0, blocking collectives: 461 us -> none  [the longest x1 430 us: run_batches(): lax.all_gather(tokens, 'ep', axis=0, tiled=True)]
    all_to_all x4 -> x7, waiting for transfers between devices: 678 us -> 992 us  [the longest x4 800 us: exchange(): return lax.all_to_all(blocks, 'ep', split_axis=0, concat_axis=0, tiled=True)]
    reduce_scatter x2 -> x1, waiting for transfers between devices: 95.3 us -> 38.2 us  [expert_mixture(): return lax.psum_scatter(sums, 'tp', scatter_dimension=1, tiled=True)]
    all_to_all x4 -> x2, local copies, waits for them, and re-layouts: 58 us -> 12.8 us  [the longest x1 12.8 us: on_device(): lax.all_to_all(send_down, 'ep', split_axis=2, concat_axis=0, tiled=True)]
    transpose x0 -> x3, local copies, waits for them, and re-layouts: none -> 43.3 us  [the longest x1 16.7 us: on_device(): back_gate_up.transpose(1, 2, 0, 3, 4).reshape((-1,) + gate_up.shape[1:])]
    unnamed x32 -> x19, local copies, waits for them, and re-layouts: 52.9 us -> 22.1 us
    all_gather x1, waiting for transfers between devices: 0.01 us -> 27.5 us  [expert_mixture(): features = lax.all_gather(features, 'tp', axis=1, tiled=True)]
    all_to_all x4 -> x7, starting transfers between devices: 24 us -> 37.2 us  [the longest x4 21.3 us: exchange(): return lax.all_to_all(blocks, 'ep', split_axis=0, concat_axis=0, tiled=True)]
  transfers between devices with their start and end apart: 7 -> 9, of which waited for: 5 -> 9; matrix products, arithmetic and copies ran while one was open for 8% -> 8% of each run, Pallas kernels for 2% -> 3%
where the time goes in v3:
time: 1290 us; the launch traced here: 1280 us
  waiting for transfers between devices  1060 us (82%)
  local copies, waits for them, and re-layouts  120 us (9%)
  starting transfers between devices  37.3 us (3%)
  Pallas kernels  32.5 us (3%)
  between operations  14.3 us (1%)
    all_to_all x4, waiting for transfers between devices, exchange(): return lax.all_to_all(blocks, 'ep', split_axis=0, concat_axis=0, tiled=True)  800 us
    all_to_all x1, waiting for transfers between devices, on_device(): lax.all_to_all(send_down, 'ep', split_axis=2, concat_axis=0, tiled=True)  167 us
    reduce_scatter x1, waiting for transfers between devices, expert_mixture(): return lax.psum_scatter(sums, 'tp', scatter_dimension=1, tiled=True)  38.2 us
    pallas_call x1, Pallas kernels, expert_sums(): pl.pallas_call(expert_body, grid=(count // block, slots), in_specs=[pl.Bl...  32.5 us
    all_gather x1, waiting for transfers between devices, expert_mixture(): features = lax.all_gather(features, 'tp', axis=1, tiled=True)  27.5 us
  transfers between devices with their start and end apart: 9, of which 9 were waited for; matrix products, arithmetic and copies ran while one was open for 8% of the time, Pallas kernels for 3%

profile of v3, /device:TPU:0, one launch (start us, length us, event | category | flops | bytes accessed | tf_op | source)
XLA Modules:
  0.0 1284.2 jit_solution(13991935976584257351)
XLA Ops:
  7.2 0.8 fusion.2
  8.0 0.8 broadcast_divide_fusion
  8.7 0.8 add_convert_fusion.2
  9.5 0.6 broadcast_in_dim.17
  10.2 7.3 all-to-all-start.1
  17.4 0.8 pad_maximum_fusion
  18.3 6.1 all-to-all-done.1
  24.3 0.9 broadcast_in_dim.16
  25.3 3.5 all-to-all-start
  29.0 18.9 %all-to-all-done = bf16[8,96,512]{2,1,0:T(8,128)(2,1)S(1)} async-done(((bf16[8,96,512]{2,1,0:T(8,128)(2,1)}), bf16[8,96,512]{2,1,0:T(8,128)(2,1)S(1)}, u32[]{:S(2)}, u32[]{:S(2)}) %all-to-all-start) | async-done | bytes 786464 | tf_op jit(solution)/shard_map/all_to_all | solution.py:70
  47.9 13.1 %copy.69 = bf16[8,256,2048]{1,0,2:T(8,128)(2,1)} copy(bf16[8,256,2048]{2,1,0:T(8,128)(2,1)} %down_ref.1) | data formatting | bytes 16777216 | tf_op jit(solution)/shard_map/optimization_barrier | solution.py:154
  61.0 5.0 all-to-all-start.2
  66.0 14.0 %copy.73 = bf16[8,8,2,256,256]{4,3,2,1,0:T(8,128)(2,1)} copy(bf16[8,8,2,256,256]{4,3,0,2,1:T(8,128)(2,1)} %bitcast.68) | data formatting | bytes 33554432 | tf_op jit(solution)/shard_map/transpose | solution.py:95
  80.0 167.5 %all-to-all-done.2 = bf16[8,256,2048]{1,0,2:T(8,128)(2,1)} async-done(((bf16[8,256,2048]{1,0,2:T(8,128)(2,1)}), bf16[8,256,2048]{1,0,2:T(8,128)(2,1)}, u32[]{:S(2)}, u32[]{:S(2)}) %all-to-all-start.2) | async-done | bytes 8388640 | tf_op jit(solution)/shard_map/all_to_all | solution.py:155
  247.5 5.7 all-to-all-start.3
  253.3 12.8 copy.71
  266.2 0.1 select_reduce_fusion
  266.3 2.2 copy.72.share_ref
  268.5 27.5 %all-gather.2.cloned.1.call-done.x_ref = bf16[768,2048]{1,0:T(8,128)(2,1)} async-done(((bf16[768,512]{1,0:T(8,128)(2,1)}), bf16[768,2048]{1,0:T(8,128)(2,1)}) %all-gather.2.cloned.1.call-update) | async-done | bytes 3145744 | tf_op jit(solution)/shard_map/all_gather | solution.py:83
  296.0 32.5 %shard_map.199 = bf16[768,2048]{1,0:T(8,128)(2,1)} custom-call(bf16[768,2048]{1,0:T(8,128)(2,1)} %all-gather.2.cloned.1.call-done.x_ref, f32[8,768,1]{2,1,0:T(8,128)} %copy.72.share_ref, bf16[8,2,2048,256]{3,2,1,0:T(8,128)(2,1)} %gate_up_ref.1, bf16[8,256,2048]{2,1,0:T(8,128)(2,1)} %down_ref.1), custom_call_target="tpu_custom_call" | custom-call | flops 19327352832 | bytes 31457280 | tf_op jit(solution)/shard_map/pallas_call | solution.py:46
  328.5 38.2 %reduce-scatter.2.cloned.1.call-done = bf16[768,512]{1,0:T(8,128)(2,1)} async-done(((bf16[768,2048]{1,0:T(8,128)(2,1)}), bf16[768,512]{1,0:T(8,128)(2,1)}) %reduce-scatter.2.cloned.1.call-update) | async-done | bytes 786448 | tf_op jit(solution)/shard_map/reduce_scatter | solution.py:85
  366.7 247.5 %all-to-all-done.3 = bf16[8,8,2,256,256]{4,3,2,1,0:T(8,128)(2,1)} async-done(((bf16[8,8,2,256,256]{4,3,2,1,0:T(8,128)(2,1)}), bf16[8,8,2,256,256]{4,3,2,1,0:T(8,128)(2,1)}, u32[]{:S(2)}, u32[]{:S(2)}) %all-to-all-start.3) | async-done | bytes 16777248 | tf_op jit(solution)/shard_map/all_to_all | solution.py:89
  614.1 4.6 all-to-all-start.4
  618.8 0.8 scatter_custom_fusion
  619.7 9.3 gather_fusion.1
  629.0 10.1 all-to-all-done.4
  639.1 5.1 all-to-all-start.6
  644.2 14.2 %gather_fusion = bf16[72,2,256,256]{3,2,1,0:T(8,128)(2,1)} fusion(bf16[64,2,256,256]{3,2,1,0:T(8,128)(2,1)} %bitcast.16, s32[1024]{0:T(1024)S(1)} %pad_clamp_fusion), kind=kCustom, calls=%fused_computation | custom fusion | bytes 37749024 | tf_op jit(solution)/shard_map/gather | solution.py:166
  658.4 190.4 %all-to-all-done.6 = bf16[8,9,256,256]{3,2,1,0:T(8,128)(2,1)} async-done(((bf16[8,9,256,256]{3,2,1,0:T(8,128)(2,1)}), bf16[8,9,256,256]{3,2,1,0:T(8,128)(2,1)}, u32[]{:S(2)}, u32[]{:S(2)}) %all-to-all-start.6) | async-done | bytes 9437216 | tf_op jit(solution)/shard_map/all_to_all | solution.py:89
  848.8 5.9 all-to-all-start.5
  854.8 8.8 copy.74
  863.6 0.2 multiply_cosine_fusion
  863.8 0.1 convert_reduce_fusion
  863.9 0.6 slice.86
  864.5 0.1 multiply_reduce_fusion.2
  864.6 6.1 psum.7
  870.8 5.6 all_gather.7
  876.4 4.8 fusion
  881.2 0.6 copy.89
  881.9 0.1 multiply_reduce_fusion
  882.0 0.1 multiply_multiply_fusion
  882.2 0.1 subtract_convert_fusion
  882.3 0.7 copy_bitcast_fusion.1
  883.0 0.7 copy_bitcast_fusion.2
  883.7 12.6 copy.79
  896.3 12.6 copy.80
  909.0 351.8 %all-to-all-done.5 = bf16[8,9,2,256,256]{4,3,2,1,0:T(8,128)(2,1)} async-done(((bf16[8,9,2,256,256]{4,3,2,1,0:T(8,128)(2,1)}), bf16[8,9,2,256,256]{4,3,2,1,0:T(8,128)(2,1)}, u32[]{:S(2)}, u32[]{:S(2)}) %all-to-all-start.5) | async-done | bytes 18874400 | tf_op jit(solution)/shard_map/all_to_all | solution.py:89
  1260.7 16.7 %copy.78 = bf16[9,2,8,256,256]{4,3,2,1,0:T(8,128)(2,1)} copy(bf16[9,2,8,256,256]{4,3,1,0,2:T(8,128)(2,1)} %bitcast.20) | data formatting | bytes 37748736 | tf_op jit(solution)/shard_map/transpose | solution.py:169
  (37 shorter events, 0.6 us)
Async XLA Ops:
  10.2 14.2 %all-to-all-start.1 = ((f32[8,96,16]{1,2,0:T(8,128)}), f32[8,96,16]{1,2,0:T(8,128)S(1)}, u32[]{:S(2)}, u32[]{:S(2)}) async-start(f32[8,96,16]{1,2,0:T(8,128)} %broadcast_in_dim.17), calls=%async_computation.1 | async-start | bytes 131072 | tf_op jit(solution)/shard_map/all_to_all | solution.py:70
  25.3 22.6 %all-to-all-start = ((bf16[8,96,512]{2,1,0:T(8,128)(2,1)}), bf16[8,96,512]{2,1,0:T(8,128)(2,1)S(1)}, u32[]{:S(2)}, u32[]{:S(2)}) async-start(bf16[8,96,512]{2,1,0:T(8,128)(2,1)} %broadcast_in_dim.16), calls=%async_computation | async-start | bytes 1572864 | tf_op jit(solution)/shard_map/all_to_all | solution.py:70
  47.9 13.1 %copy-start = (bf16[8,96,512]{2,1,0:T(8,128)(2,1)}, bf16[8,96,512]{2,1,0:T(8,128)(2,1)S(1)}, u32[]{:S(2)}) copy-start(bf16[8,96,512]{2,1,0:T(8,128)(2,1)S(1)} %all-to-all-done) | copy-start | bytes 2359300
  61.0 186.5 %all-to-all-start.2 = ((bf16[8,256,2048]{1,0,2:T(8,128)(2,1)}), bf16[8,256,2048]{1,0,2:T(8,128)(2,1)}, u32[]{:S(2)}, u32[]{:S(2)}) async-start(bf16[8,256,2048]{1,0,2:T(8,128)(2,1)} %copy.69), calls=%async_computation.2 | async-start | bytes 16777216 | tf_op jit(solution)/shard_map/all_to_all | solution.py:155
  247.5 366.7 %all-to-all-start.3 = ((bf16[8,8,2,256,256]{4,3,2,1,0:T(8,128)(2,1)}), bf16[8,8,2,256,256]{4,3,2,1,0:T(8,128)(2,1)}, u32[]{:S(2)}, u32[]{:S(2)}) async-start(bf16[8,8,2,256,256]{4,3,2,1,0:T(8,128)(2,1)} %copy.73), calls=%async_computation.4 | async-start | bytes 33554432 | tf_op jit(solution)/shard_map/all_to_all | solution.py:89
  253.2 12.9 %copy-start.5 = (s32[64]{0:T(128)S(1)}, s32[64]{0:T(128)}, u32[]{:S(2)}) copy-start(s32[64]{0:T(128)} %param.23) | copy-start | bytes 772
  253.2 42.8 %all-gather.2.cloned.1.call-start = ((), (), s32[]{:S(2)}) async-start(), calls=%async_computation.8 | async-start | bytes 3932160 | tf_op jit(solution)/shard_map/all_gather | solution.py:83
  266.1 100.6 %reduce-scatter.2.cloned.1.call-start = ((), (), s32[]{:S(2)}) async-start(), calls=%async_computation.9 | async-start | bytes 3932160 | tf_op jit(solution)/shard_map/reduce_scatter | solution.py:85
  268.5 351.0 %copy-start.6 = (s32[72]{0:T(128)S(1)}, s32[72]{0:T(128)}, u32[]{:S(2)}) copy-start(s32[72]{0:T(128)} %param.24) | copy-start | bytes 868
  614.1 25.0 %all-to-all-start.4 = ((bf16[8,96,512]{2,1,0:T(8,128)(2,1)}), bf16[8,96,512]{2,1,0:T(8,128)(2,1)S(1)}, u32[]{:S(2)}, u32[]{:S(2)}) async-start(bf16[8,96,512]{2,1,0:T(8,128)(2,1)} %bitcast.70), calls=%async_computation.5 | async-start | bytes 1572864 | tf_op jit(solution)/shard_map/all_to_all | solution.py:89
  639.1 209.7 %all-to-all-start.6 = ((bf16[8,9,256,256]{3,2,1,0:T(8,128)(2,1)}), bf16[8,9,256,256]{3,2,1,0:T(8,128)(2,1)}, u32[]{:S(2)}, u32[]{:S(2)}) async-start(bf16[8,9,256,256]{3,2,1,0:T(8,128)(2,1)} %bitcast.64), calls=%async_computation.7 | async-start | bytes 18874368 | tf_op jit(solution)/shard_map/all_to_all | solution.py:89
  848.8 411.9 %all-to-all-start.5 = ((bf16[8,9,2,256,256]{4,3,2,1,0:T(8,128)(2,1)}), bf16[8,9,2,256,256]{4,3,2,1,0:T(8,128)(2,1)}, u32[]{:S(2)}, u32[]{:S(2)}) async-start(bf16[8,9,2,256,256]{4,3,2,1,0:T(8,128)(2,1)} %bitcast.62), calls=%async_computation.6 | async-start | bytes 37748736 | tf_op jit(solution)/shard_map/all_to_all | solution.py:89
  854.7 8.8 copy-start.7
  854.8 9.8 copy-start.1
  854.8 15.9 %copy-start.2 = (f32[512]{0:T(512)S(1)}, f32[512]{0:T(512)}, u32[]{:S(2)}) copy-start(f32[512]{0:T(512)} %param.27) | copy-start | bytes 6148
  854.8 27.2 %copy-start.3 = (f32[128]{0:T(128)S(1)}, f32[128]{0:T(128)}, u32[]{:S(2)}) copy-start(f32[128]{0:T(128)} %param.30) | copy-start | bytes 1540
  854.8 27.2 %copy-start.4 = (f32[128]{0:T(128)S(1)}, f32[128]{0:T(128)}, u32[]{:S(2)}) copy-start(f32[128]{0:T(128)} %param.29) | copy-start | bytes 1540
Sparse Core Ops, SparseCore 0:
  266.2 29.7 all-gather.1
  328.6 38.0 reduce-scatter.1
